TPU v7x, 32 devices: a whole 2x2x4 slice. The times are simulated.
32 devices in a mesh: grp: 4 (over y, x), dev: 8 (over z, core).
Axes of the slice: x: 2, y: 2, z: 4, core: 2. Of those that a mesh axis runs over, the one named last changes fastest.
Arguments:
- queries: bfloat16 [4096, 256], P(('grp', 'dev')), may hold values from -32 to 32
- items: bfloat16 [4096, 256], P(('grp', 'dev')), may hold values from -24 to 24
- item_ids: int32 [4096], P('grp'), may hold values from 0 to 262143
- neg_embed: bfloat16 [4096, 256], P('dev'), may hold values from -6 to 6
- neg_logq: float32 [4096], P('dev'), may hold values from -12 to -8
- logq_table: float32 [262144], replicated, may hold values from -11 to -9.5
Outputs:
- query_loss: float32 [4096], P(('grp', 'dev'))
- query_grad: float32 [4096, 256], P(('grp', 'dev'))
- item_grad: float32 [4096, 256], P(('grp', 'dev'))
- negative_grad: float32 [4096, 256], P('dev')
Inputs may be any that keep to these rules, and one draw needn't show every extreme that they name: `item_ids`: a row of logq_table.
All inputs are finite; a program needn't handle non-finite values.
Results may differ from a plain program's by a relative error of at most 0.0036.
Values may be sent and summed in bfloat16 or wider, within the bound.
No kernel may reach another device: no remote copies, remote signals or barrier semaphores. Data moves between devices by JAX's collectives and lax.ppermute only.
A program may use at most 64 MiB of HBM per device.

v0:
```python
import jax
import jax.numpy as jnp
from jax import lax
from jax.sharding import PartitionSpec as P

logit_scale = 0.25


def block_shape(all_rows):
    block_rows = min(512, all_rows)
    return (block_rows, all_rows // block_rows)


def log_total(maxima, totals):
    row_max = lax.pmax(maxima, "dev")
    row_sum = lax.psum(totals * jnp.exp(maxima - row_max), "dev")
    return row_max + jnp.log(row_sum)


def row_stats(scores):
    row_max = jnp.max(scores, axis=1)
    return (row_max, jnp.sum(jnp.exp(scores - row_max[:, None]), axis=1))


def logits(q_block, candidates, cand_offsets):
    return (
        logit_scale * jnp.dot(q_block, candidates.T, preferred_element_type=jnp.float32)
        - cand_offsets[None, :]
    )


def local(queries, items, item_ids, neg_embed, neg_logq, logq_table):
    own_rows, feat_width = queries.shape
    dev_index = lax.axis_index("dev")
    own_start = dev_index * own_rows
    own_ids = lax.dynamic_slice_in_dim(item_ids, own_start, own_rows, 0)
    own_offsets = jnp.take(logq_table, own_ids, axis=0)
    group_q = lax.all_gather(queries, "dev", axis=0, tiled=True)
    all_rows = group_q.shape[0]
    block_rows, block_count = block_shape(all_rows)
    blocks = group_q.reshape(block_count, block_rows, feat_width)
    starts = jnp.arange(block_count, dtype=jnp.int32) * block_rows
    candidates = jnp.concatenate([items, neg_embed], axis=0)
    cand_offsets = jnp.concatenate([own_offsets, neg_logq], axis=0)
    columns = jnp.arange(candidates.shape[0], dtype=jnp.int32)

    def positives(first_row):
        targets = first_row + jnp.arange(block_rows, dtype=jnp.int32) - own_start
        return (columns[None, :] == targets[:, None]) & (columns[None, :] < own_rows)

    def forward(packed):
        q_block, first_row = packed
        scores = logits(q_block, candidates, cand_offsets)
        row_max, row_sum = row_stats(scores)
        return (row_max, row_sum, jnp.sum(jnp.where(positives(first_row), scores, 0.0), axis=1))

    maxima, totals, matched = lax.map(forward, (blocks, starts))
    log_norm = log_total(maxima.reshape(all_rows), totals.reshape(all_rows))
    own_norm = lax.dynamic_slice_in_dim(log_norm, own_start, own_rows, 0)
    own_match = lax.dynamic_slice_in_dim(matched.reshape(all_rows), own_start, own_rows, 0)
    query_loss = own_norm - own_match

    def backward(summed, packed):
        q_block, first_row, block_norm = packed
        scores = logits(q_block, candidates, cand_offsets)
        logit_grad = (
            logit_scale
            * (jnp.exp(scores - block_norm[:, None]) - positives(first_row).astype(jnp.float32))
        ).astype(jnp.bfloat16)
        summed = summed + jnp.einsum(
            "rc,rd->cd", logit_grad, q_block, preferred_element_type=jnp.float32
        )
        return (summed, jnp.dot(logit_grad, candidates, preferred_element_type=jnp.float32))

    zero_acc = jnp.zeros((candidates.shape[0], feat_width), jnp.float32)
    cand_grad, q_partial = lax.scan(
        backward, zero_acc, (blocks, starts, log_norm.reshape(block_count, block_rows))
    )
    query_grad = lax.psum_scatter(
        q_partial.reshape(all_rows, feat_width), "dev", scatter_dimension=0, tiled=True
    )
    item_grad = cand_grad[:own_rows]
    negative_part = cand_grad[own_rows:]
    negative_grad = lax.psum(negative_part, "grp")
    return (query_loss, query_grad, item_grad, negative_grad)


def solution(mesh):
    return jax.shard_map(
        local,
        mesh=mesh,
        in_specs=(
            P(("grp", "dev"), None),
            P(("grp", "dev"), None),
            P("grp"),
            P("dev", None),
            P("dev"),
            P(),
        ),
        out_specs=(
            P(("grp", "dev")),
            P(("grp", "dev"), None),
            P(("grp", "dev"), None),
            P("dev", None),
        ),
        check_vma=False,
    )
```

profile of v0, /device:TPU:0, one launch (start us, length us, event | category | flops | bytes accessed | tf_op | source)
XLA Modules:
  0.0 128.1 jit_solution(7890898230688318742)
XLA Ops:
  8.1 0.8 compare_select_fusion
  9.2 1.1 gather_fusion
  10.4 0.8 and_select_fusion
  11.2 0.8 constant_dynamic-update-slice_fusion.1
  12.0 16.7 %all_gather.3 = bf16[1024,256]{1,0:T(8,128)(2,1)S(1)} all-gather(bf16[128,256]{1,0:T(8,128)(2,1)} %param.10), channel_id=1, replica_groups=mesh['grp'=4,'dev'=8] {'dev'}, dimensions={0}, use_global_device_ids=true | all-gather | bytes 589824 | tf_op jit(solution)/shard_map/all_gather | solution.py:38
  28.7 0.7 pad_maximum_fusion
  29.4 5.2 %while.30 = (s32[]{:T(128)}, f32[2,512]{1,0:T(2,128)S(1)}, f32[2,512]{1,0:T(2,128)S(1)}, f32[2,512]{1,0:T(2,128)S(1)}, bf16[2,512,256]{2,1,0:T(8,128)(2,1)S(1)},...) while((s32[]{:T(128)}, f32[2,512]{1,0:T(2,128)S(1)}, ...), condition=%wide.region_4.5_spmd.clone.clone, body=%wide.region_0.4_spmd.clone.clone.sunk | while | flops 170721408 | bytes 3241369 | solution.py:57
  29.4 0.6 dynamic_slice.67
  30.0 0.6 add_subtract_fusion.4
  31.2 0.7 select_reduce_fusion.2
  32.0 0.6 dynamic_slice.67
  32.6 0.6 add_subtract_fusion.4
  33.8 0.7 select_reduce_fusion.2
  34.6 17.0 %pmax.7 = f32[1024]{0:T(1024)S(1)} all-reduce(f32[1024]{0:T(1024)S(1)} %bitcast.69), channel_id=1, replica_groups=mesh['grp'=4,'dev'=8] {'dev'}, use_global_device_ids=true, to_apply=%region_5.6 | all-reduce | flops 1024 | bytes 8192 | tf_op jit(solution)/shard_map/pmax | solution.py:15
  51.6 13.6 %psum.14 = f32[1024]{0:T(1024)S(1)} all-reduce(f32[1024]{0:T(1024)S(1)} %exponential_multiply_fusion), channel_id=1, replica_groups=mesh['grp'=4,'dev'=8] {'dev'}, use_global_device_ids=true, to_apply=%region_6.7 | all-reduce | flops 1024 | bytes 8192 | tf_op jit(solution)/shard_map/psum | solution.py:16
  65.2 9.0 %while.31 = (s32[]{:T(128)}, f32[640,256]{1,0:T(8,128)S(1)}, f32[2,512,256]{2,1,0:T(8,128)}, bf16[2,512,256]{2,1,0:T(8,128)(2,1)S(1)}, bf16[640,256]{1,0:T(8,128...) while((s32[]{:T(128)}, f32[640,256]{1,0:T(8,128)S(1)}, ...), condition=%wide.region_8.9_spmd.clone.clone, body=%wide.region_7.8_spmd.clone.clone.sunk | while | flops 506594944 | bytes 13385563 | solution.py:76
  65.2 0.6 dynamic_slice.71
  65.8 0.6 add_subtract_fusion.5
  66.5 0.6 fusion.47
  67.7 0.7 copy-done.1
  68.7 1.0 copy-done.2
  69.7 0.6 dynamic_slice.71
  70.3 0.6 add_subtract_fusion.5
  71.0 0.6 fusion.47
  71.6 0.5 convolution_add_fusion.2
  72.2 0.7 copy-done.1
  73.2 1.0 copy-done.2
  74.2 0.8 slice.7
  75.7 0.7 slice.6
  76.3 0.6 dynamic-slice_subtract_fusion
  76.9 41.9 %all-reduce.2.cloned.1.call-done = f32[512,256]{1,0:T(8,128)} async-done(((f32[512,256]{1,0:T(8,128)}), f32[512,256]{1,0:T(8,128)}) %all-reduce.2.cloned.1.call-update) | async-done | bytes 524304 | tf_op jit(solution)/shard_map/psum | solution.py:84
  118.8 1.9 %copy.40 = f32[512,256]{1,0:T(8,128)} copy(f32[512,256]{1,0:T(8,128)} %all-reduce.2.cloned.1.call-done) | data formatting | bytes 1048576
  (44 shorter events, 3.5 us)
Async XLA Ops:
  8.0 1.2 copy-start
  8.0 21.4 %copy-start.3 = (bf16[512,256]{1,0:T(8,128)(2,1)S(1)}, bf16[512,256]{1,0:T(8,128)(2,1)}, u32[]{:S(2)}) copy-start(bf16[512,256]{1,0:T(8,128)(2,1)} %param.13) | copy-start | bytes 786436
  8.0 110.8 %all-reduce.2.cloned.1.call-start = ((), (), s32[]{:S(2)}) async-start(), calls=%async_computation.2 | async-start | bytes 1048576 | tf_op jit(solution)/shard_map/psum | solution.py:84
  67.1 1.2 copy-start.1
  68.7 1.0 copy-start.2
  71.6 1.2 copy-start.1
  73.2 1.0 copy-start.2
  75.1 43.7 %reduce-scatter.2.cloned.1.call-start = ((), (), s32[]{:S(2)}) async-start(), calls=%async_computation.1 | async-start | bytes 1179648 | tf_op jit(solution)/shard_map/reduce_scatter | solution.py:79
Sparse Core Ops, SparseCore 0:
  75.2 43.5 all-reduce.1
Sparse Core Ops, SparseCore 1:
  78.4 30.7 reduce-scatter.1
where the time goes:
time: 129 us; the launch traced here: 128 us
  blocking collectives  47.3 us (37%)
  waiting for transfers between devices  42.4 us (33%)
  between operations  15.6 us (12%)
  local copies, waits for them, and re-layouts  11.6 us (9%)
  other arithmetic  6.94 us (5%)
  matrix products  4.02 us (3%)
    psum x1, waiting for transfers between devices, local(): negative_grad = lax.psum(negative_part, 'grp')  41.9 us
    pmax x1, blocking collectives, log_total(): row_max = lax.pmax(maxima, 'dev')  17 us
    all_gather x1, blocking collectives, local(): group_q = lax.all_gather(queries, 'dev', axis=0, tiled=True)  16.7 us
    psum x1, blocking collectives, log_total(): row_sum = lax.psum(totals * jnp.exp(maxima - row_max), 'dev')  13.6 us
    while x8, local copies, waits for them, and re-layouts  3.35 us
    unnamed x9, local copies, waits for them, and re-layouts  2.99 us
    sub x4, other arithmetic, positives(): targets = first_row + jnp.arange(block_rows, dtype=jnp.int32) - own_start  2.59 us
  transfers between devices with their start and end apart: 2, of which 1 were waited for; matrix products, arithmetic and copies ran while one was open for 1% of the time, Pallas kernels for 0%

commit v1 on v0

--- a/solution.py
+++ b/solution.py
@@ -81,7 +81,11 @@
     )
     item_grad = cand_grad[:own_rows]
     negative_part = cand_grad[own_rows:]
-    negative_grad = lax.psum(negative_part, "grp")
+
+    def begin_the_shelves(load):
+        return lax.all_gather(load, axis_name="grp").sum(axis=0)
+
+    negative_grad = begin_the_shelves(negative_part)
     return (query_loss, query_grad, item_grad, negative_grad)
 
 

time: 129 us -> 119 us (0.922)
  waiting for transfers between devices: 42.4 us -> 32.2 us
  other arithmetic: 6.94 us -> 9.54 us
  local copies, waits for them, and re-layouts: 11.6 us -> 9.74 us
    psum x1 -> x0, waiting for transfers between devices: 41.9 us -> none  [local(): negative_grad = lax.psum(negative_part, 'grp')]
    all_gather x0 -> x1, waiting for transfers between devices: none -> 31.7 us  [begin_the_shelves(): return lax.all_gather(load, axis_name='grp').sum(axis=0)]
    reduce_sum x0 -> x1, other arithmetic: none -> 2.6 us  [begin_the_shelves(): return lax.all_gather(load, axis_name='grp').sum(axis=0)]
    unnamed x9 -> x8, local copies, waits for them, and re-layouts: 2.99 us -> 1.12 us
  transfers between devices with their start and end apart: 2 -> 2, of which waited for: 1 -> 1; matrix products, arithmetic and copies ran while one was open for 1% -> 3% of each run, Pallas kernels for 0% -> 0%
where the time goes in v1:
time: 119 us
  blocking collectives  47.3 us (40%)
  waiting for transfers between devices  32.2 us (27%)
  between operations  15.6 us (13%)
  local copies, waits for them, and re-layouts  9.74 us (8%)
  other arithmetic  9.54 us (8%)
  matrix products  4.02 us (3%)
    all_gather x1, waiting for transfers between devices, begin_the_shelves(): return lax.all_gather(load, axis_name='grp').sum(axis=0)  31.7 us
    pmax x1, blocking collectives, log_total(): row_max = lax.pmax(maxima, 'dev')  17 us
    all_gather x1, blocking collectives, local(): group_q = lax.all_gather(queries, 'dev', axis=0, tiled=True)  16.7 us
    psum x1, blocking collectives, log_total(): row_sum = lax.psum(totals * jnp.exp(maxima - row_max), 'dev')  13.6 us
    while x8, local copies, waits for them, and re-layouts  3.34 us
    reduce_sum x1, other arithmetic, begin_the_shelves(): return lax.all_gather(load, axis_name='grp').sum(axis=0)  2.6 us
    sub x4, other arithmetic, positives(): targets = first_row + jnp.arange(block_rows, dtype=jnp.int32) - own_start  2.59 us
  transfers between devices with their start and end apart: 2, of which 1 were waited for; matrix products, arithmetic and copies ran while one was open for 3% of the time, Pallas kernels for 0%

profile of v1, /device:TPU:0, one launch (start us, length us, event | category | flops | bytes accessed | tf_op | source)
XLA Modules:
  0.0 118.6 jit_solution(369046078729853366)
XLA Ops:
  8.1 0.8 compare_select_fusion
  9.2 1.1 gather_fusion
  10.4 0.8 and_select_fusion
  11.2 0.8 constant_dynamic-update-slice_fusion.1
  12.0 16.7 %all_gather.9 = bf16[1024,256]{1,0:T(8,128)(2,1)S(1)} all-gather(bf16[128,256]{1,0:T(8,128)(2,1)} %param.10), channel_id=1, replica_groups=mesh['grp'=4,'dev'=8] {'dev'}, dimensions={0}, use_global_device_ids=true | all-gather | bytes 589824 | tf_op jit(solution)/shard_map/all_gather | solution.py:38
  28.7 0.7 pad_maximum_fusion
  29.4 5.2 %while.30 = (s32[]{:T(128)}, f32[2,512]{1,0:T(2,128)S(1)}, f32[2,512]{1,0:T(2,128)S(1)}, f32[2,512]{1,0:T(2,128)S(1)}, bf16[2,512,256]{2,1,0:T(8,128)(2,1)S(1)},...) while((s32[]{:T(128)}, f32[2,512]{1,0:T(2,128)S(1)}, ...), condition=%wide.region_4.5_spmd.clone.clone, body=%wide.region_0.4_spmd.clone.clone.sunk | while | flops 170721408 | bytes 3241369 | solution.py:57
  29.4 0.6 dynamic_slice.67
  30.0 0.6 add_subtract_fusion.4
  31.2 0.7 select_reduce_fusion.2
  32.0 0.6 dynamic_slice.67
  32.6 0.6 add_subtract_fusion.4
  33.8 0.7 select_reduce_fusion.2
  34.6 17.0 %pmax.7 = f32[1024]{0:T(1024)S(1)} all-reduce(f32[1024]{0:T(1024)S(1)} %bitcast.71), channel_id=1, replica_groups=mesh['grp'=4,'dev'=8] {'dev'}, use_global_device_ids=true, to_apply=%region_5.6 | all-reduce | flops 1024 | bytes 8192 | tf_op jit(solution)/shard_map/pmax | solution.py:15
  51.6 13.6 %psum.7 = f32[1024]{0:T(1024)S(1)} all-reduce(f32[1024]{0:T(1024)S(1)} %exponential_multiply_fusion), channel_id=1, replica_groups=mesh['grp'=4,'dev'=8] {'dev'}, use_global_device_ids=true, to_apply=%region_6.7 | all-reduce | flops 1024 | bytes 8192 | tf_op jit(solution)/shard_map/psum | solution.py:16
  65.2 9.0 %while.31 = (s32[]{:T(128)}, f32[640,256]{1,0:T(8,128)S(1)}, f32[2,512,256]{2,1,0:T(8,128)}, bf16[2,512,256]{2,1,0:T(8,128)(2,1)S(1)}, bf16[640,256]{1,0:T(8,128...) while((s32[]{:T(128)}, f32[640,256]{1,0:T(8,128)S(1)}, ...), condition=%wide.region_8.9_spmd.clone.clone, body=%wide.region_7.8_spmd.clone.clone.sunk | while | flops 506594944 | bytes 13385563 | solution.py:76
  65.2 0.6 dynamic_slice.71
  65.8 0.6 add_subtract_fusion.5
  66.5 0.6 fusion.47
  67.7 0.7 copy-done.1
  68.7 1.0 copy-done.2
  69.7 0.6 dynamic_slice.71
  70.3 0.6 add_subtract_fusion.5
  71.0 0.6 fusion.47
  71.6 0.5 convolution_add_fusion.2
  72.2 0.7 copy-done.1
  73.2 1.0 copy-done.2
  74.2 0.8 slice.7
  75.6 0.7 slice.6
  76.3 0.6 dynamic-slice_subtract_fusion
  76.9 31.7 %all-gather.3.cloned.1.call-done = f32[2048,256]{1,0:T(8,128)} async-done(((f32[512,256]{1,0:T(8,128)}), f32[2048,256]{1,0:T(8,128)}) %all-gather.3.cloned.1.call-update) | async-done | bytes 2097168 | tf_op jit(solution)/shard_map/all_gather | solution.py:86
  108.6 2.6 %reduce_sum.27 = f32[512,256]{1,0:T(8,128)} reduce(f32[4,512,256]{2,1,0:T(8,128)} %bitcast.65, f32[]{:T(128)} %constant.41.clone.1), dimensions={0}, to_apply=%region_10.11 | reduce | flops 393216 | bytes 2621444 | tf_op jit(solution)/shard_map/reduce_sum | solution.py:86
  (44 shorter events, 3.5 us)
Async XLA Ops:
  8.0 1.2 %copy-start = (f32[262144]{0:T(1024)S(1)}, f32[262144]{0:T(1024)}, u32[]{:S(2)}) copy-start(f32[262144]{0:T(1024)} %param.15) | copy-start | bytes 3145732
  8.0 21.4 %copy-start.3 = (bf16[512,256]{1,0:T(8,128)(2,1)S(1)}, bf16[512,256]{1,0:T(8,128)(2,1)}, u32[]{:S(2)}) copy-start(bf16[512,256]{1,0:T(8,128)(2,1)} %param.13) | copy-start | bytes 786436
  8.0 100.6 %all-gather.3.cloned.1.call-start = ((), (), s32[]{:S(2)}) async-start(), calls=%async_computation.2 | async-start | bytes 2621440 | tf_op jit(solution)/shard_map/all_gather | solution.py:86
  67.1 1.2 %copy-start.1 = (f32[2,512,256]{2,1,0:T(8,128)S(1)}, f32[2,512,256]{2,1,0:T(8,128)}, u32[]{:S(2)}) copy-start(f32[2,512,256]{2,1,0:T(8,128)} %get-tuple-element.426) | copy-start | bytes 3145732 | tf_op jit(solution)/shard_map/while
  68.7 1.0 copy-start.2
  71.6 1.2 %copy-start.1 = (f32[2,512,256]{2,1,0:T(8,128)S(1)}, f32[2,512,256]{2,1,0:T(8,128)}, u32[]{:S(2)}) copy-start(f32[2,512,256]{2,1,0:T(8,128)} %get-tuple-element.426) | copy-start | bytes 3145732 | tf_op jit(solution)/shard_map/while
  73.2 1.0 copy-start.2
  75.1 36.1 %reduce-scatter.2.cloned.1.call-start = ((), (), s32[]{:S(2)}) async-start(), calls=%async_computation.1 | async-start | bytes 1179648 | tf_op jit(solution)/shard_map/reduce_scatter | solution.py:79
Sparse Core Ops, SparseCore 0:
  75.2 33.3 all-gather.2
Sparse Core Ops, SparseCore 1:
  78.4 30.8 reduce-scatter.1
